TPU v7x, 32 devices: a whole 2x2x4 slice. The times are simulated.
32 devices in a mesh: rows: 16 (over z, y, x), rep: 2 (over core).
Axes of the slice: x: 2, y: 2, z: 4, core: 2. Of those that a mesh axis runs over, the one named last changes fastest.
Arguments:
- grad_out: bfloat16 [2048, 1024], P('rows'), may hold values from -8 to 8
- w_self: bfloat16 [1024, 1024], replicated, may hold values from -0.1875 to 0.1875
- w_neigh: bfloat16 [1024, 1024], replicated, may hold values from -0.1875 to 0.1875
- adj_tiles: bfloat16 [16, 8, 128, 128], P('rows'), may hold values from -0.3125 to 0.3125
- tile_index: int32 [16, 8], P('rows'), may hold values from 0 to 15, as said below
- tile_count: int32 [16], P('rows'), may hold values from 4 to 8, as said below
- prompt_ids: int32 [2048], P('rows'), may hold values from 0 to 15
Outputs:
- input_grad: bfloat16 [2048, 1024], P('rows')
- prompt_grad: float32 [16, 1024], replicated
Inputs may be any that keep to these rules, and one draw needn't show every extreme that they name: `tile_index`: each row holds 8 different tile numbers; only the first tile_count entries of a row are used. `tile_count`: some destination tile uses all 8 slots.
All inputs are finite; a program needn't handle non-finite values.
Results may differ from a plain program's by a relative error of at most 0.0041.
Values may be sent and summed in bfloat16 or wider, within the bound.
A program may use at most 64 MiB of HBM per device.

v0:
```python
import math

import jax
import jax.numpy as jnp
from jax import lax
from jax.sharding import PartitionSpec as P

PROMPTS = 16


def shards(grad_out, w_self, w_neigh, adj_tiles, tile_index, tile_count, prompt_ids):
    rows_dev, width = grad_out.shape
    local_tiles, max_slots, tile_size, _ = adj_tiles.shape
    n_rows = lax.axis_size("rows")
    n_rep = lax.axis_size("rep")
    rep_index = lax.axis_index("rep")
    total_tiles = local_tiles * n_rows
    slot_ids = jnp.arange(max_slots)
    in_use = slot_ids[None, :] < tile_count[:, None]
    matches = (tile_index[:, :, None] == jnp.arange(total_tiles)[None, None, :]) & in_use[
        :, :, None
    ]
    present = jnp.any(matches, axis=1)
    slot_table = jnp.argmax(matches, axis=1)
    contract = (((1,), (1,)), ((), ()))
    half_rows = rows_dev // n_rep
    mine = lax.dynamic_slice_in_dim(grad_out, rep_index * half_rows, half_rows, 0)
    initial = jnp.zeros((local_tiles, tile_size, width), jnp.float32)

    def half_column(place):
        return place // half_rows * rows_dev + rep_index * half_rows + place % half_rows

    piece = lax.all_gather(mine, "rows", axis=0, tiled=True)
    piece_rows = piece.shape[0]
    unit = math.gcd(math.gcd(piece_rows, tile_size), half_rows)
    segments = piece_rows // unit
    feat = piece.shape[1]

    def one_segment(index, carry):
        start = index * unit
        rows_part = lax.dynamic_slice_in_dim(piece, start, unit, 0)
        column = half_column(start)
        source = column // tile_size
        offset = column % tile_size
        slot = slot_table[0, source]
        zero = jnp.zeros((), jnp.int32)
        block = lax.dynamic_slice(
            adj_tiles, (jnp.int32(0), slot, zero, offset), (1, 1, tile_size, unit)
        )
        block = block.reshape(tile_size, unit)

        def product(args):
            blk, part_rows = args
            return jnp.dot(blk, part_rows, preferred_element_type=jnp.float32)

        def nothing(args):
            return jnp.zeros((tile_size, feat), jnp.float32)

        term = lax.cond(present[0, source], product, nothing, (block, rows_part))
        updated = [carry[0] + term]
        return jnp.stack(updated, axis=0)

    partial_value = lax.fori_loop(0, segments, one_segment, initial)
    summed = lax.psum(partial_value.reshape(rows_dev, width), "rep")
    aggregate = summed.astype(jnp.bfloat16)
    full_grad = lax.dot_general(grad_out, w_self, contract, preferred_element_type=jnp.float32)
    full_grad = full_grad + lax.dot_general(
        aggregate, w_neigh, contract, preferred_element_type=jnp.float32
    )
    onehot = (prompt_ids[None, :] == jnp.arange(PROMPTS)[:, None]).astype(jnp.float32)
    prompt_part = jnp.dot(onehot, full_grad, precision=lax.Precision.HIGHEST)
    prompt_grad = lax.psum(prompt_part, "rows")
    return (full_grad.astype(jnp.bfloat16), prompt_grad)


def solution(mesh):
    placed = (
        P("rows", None),
        P(),
        P(),
        P("rows", None, None, None),
        P("rows", None),
        P("rows"),
        P("rows"),
    )
    return jax.shard_map(
        shards, mesh=mesh, in_specs=placed, out_specs=(P("rows", None), P()), check_vma=False
    )
```

profile of v0, /device:TPU:0, one launch (start us, length us, event | category | flops | bytes accessed | tf_op | source)
XLA Modules:
  0.0 250.4 jit_solution(9167569189331557641)
XLA Ops:
  7.2 1.7 constant_dynamic-slice_fusion.2
  9.7 0.7 fusion.10
  10.4 1.3 iota_reduce_fusion
  11.7 3.3 %fusion.13 = f32[128,1024]{1,0:T(8,128)} fusion(bf16[128,1024]{1,0:T(8,128)(2,1)} %param.11, bf16[1024,1024]{1,0:T(8,128)(2,1)} %param.12), kind=kOutput, calls=%fused_computation.22 | convolution fusion | flops 268435456 | bytes 2883584 | tf_op jit(solution)/shard_map/dot_general | solution.py:66
  15.0 59.5 %all-gather.2.cloned.1.call-done = bf16[1024,1024]{1,0:T(8,128)(2,1)} async-done(((bf16[64,1024]{1,0:T(8,128)(2,1)}), bf16[1024,1024]{1,0:T(8,128)(2,1)}) %all-gather.2.cloned.1.call-update) | async-done | bytes 2097168 | tf_op jit(solution)/shard_map/all_gather | solution.py:33
  74.5 49.8 %while.16 = (s32[]{:T(128)}, f32[1,128,1024]{2,1,0:T(8,128)S(1)}, s32[]{:T(128)}, pred[1,16]{1,0:T(4,128)(4,1)S(1)}, s32[1,16]{1,0:T(1,128)S(1)}, /*index=5*/bf1...) while((s32[]{:T(128)}, f32[1,128,1024]{2,1,0:T(8,128)S(1)}, ...), condition=%wide.region_5.6_spmd, body=%wide.region_2.5_spmd.sunk | while | flops 16908344 | bytes 2261804 | solution.py:63
  74.6 0.7 fusion.21
  75.3 0.8 conditional.2
  76.2 0.7 fusion.21
  76.9 4.7 %conditional.2 = (f32[128,1024]{1,0:T(8,128)S(1)}) conditional(s32[]{:T(128)} %bitcast.25, () %tuple.66, (s32[1,16]{1,0:T(1,128)S(1)}, s32[]{:T(128)}, s32[]{:T(128)}, bf16[1,8,128,128]{3,2,1,0:T(8,128)(2,1)}, s32[]{:T(128)}, /*index=5*/pred[]{:T(512)}, bf16[1024,1024]{1,0:T(8,128)(2,1)}) %tuple.67), branch_computations={%region_3.3_spmd, %region_4.4_spmd} | conditional | flops 16777228 | bytes 688299 | solution.py:59
  77.6 0.7 constant_dynamic-slice_fusion
  80.4 1.2 fusion
  81.8 0.7 fusion.21
  82.5 0.8 conditional.2
  83.4 0.7 fusion.21
  84.1 4.7 %conditional.2 = (f32[128,1024]{1,0:T(8,128)S(1)}) conditional(s32[]{:T(128)} %bitcast.25, () %tuple.66, (s32[1,16]{1,0:T(1,128)S(1)}, s32[]{:T(128)}, s32[]{:T(128)}, bf16[1,8,128,128]{3,2,1,0:T(8,128)(2,1)}, s32[]{:T(128)}, /*index=5*/pred[]{:T(512)}, bf16[1024,1024]{1,0:T(8,128)(2,1)}) %tuple.67), branch_computations={%region_3.3_spmd, %region_4.4_spmd} | conditional | flops 16777228 | bytes 688299 | solution.py:59
  84.8 0.7 constant_dynamic-slice_fusion
  87.6 1.2 fusion
  89.7 0.8 conditional.2
  90.6 0.7 fusion.21
  91.3 0.8 conditional.2
  92.3 0.7 fusion.21
  92.9 0.8 conditional.2
  94.6 4.7 %conditional.2 = (f32[128,1024]{1,0:T(8,128)S(1)}) conditional(s32[]{:T(128)} %bitcast.25, () %tuple.66, (s32[1,16]{1,0:T(1,128)S(1)}, s32[]{:T(128)}, s32[]{:T(128)}, bf16[1,8,128,128]{3,2,1,0:T(8,128)(2,1)}, s32[]{:T(128)}, /*index=5*/pred[]{:T(512)}, bf16[1024,1024]{1,0:T(8,128)(2,1)}) %tuple.67), branch_computations={%region_3.3_spmd, %region_4.4_spmd} | conditional | flops 16777228 | bytes 688299 | solution.py:59
  95.3 0.7 constant_dynamic-slice_fusion
  98.1 1.2 fusion
  100.2 0.8 conditional.2
  101.1 0.7 fusion.21
  101.8 4.7 %conditional.2 = (f32[128,1024]{1,0:T(8,128)S(1)}) conditional(s32[]{:T(128)} %bitcast.25, () %tuple.66, (s32[1,16]{1,0:T(1,128)S(1)}, s32[]{:T(128)}, s32[]{:T(128)}, bf16[1,8,128,128]{3,2,1,0:T(8,128)(2,1)}, s32[]{:T(128)}, /*index=5*/pred[]{:T(512)}, bf16[1024,1024]{1,0:T(8,128)(2,1)}) %tuple.67), branch_computations={%region_3.3_spmd, %region_4.4_spmd} | conditional | flops 16777228 | bytes 688299 | solution.py:59
  102.5 0.7 constant_dynamic-slice_fusion
  105.3 1.2 fusion
  107.4 0.8 conditional.2
  109.0 4.7 %conditional.2 = (f32[128,1024]{1,0:T(8,128)S(1)}) conditional(s32[]{:T(128)} %bitcast.25, () %tuple.66, (s32[1,16]{1,0:T(1,128)S(1)}, s32[]{:T(128)}, s32[]{:T(128)}, bf16[1,8,128,128]{3,2,1,0:T(8,128)(2,1)}, s32[]{:T(128)}, /*index=5*/pred[]{:T(512)}, bf16[1024,1024]{1,0:T(8,128)(2,1)}) %tuple.67), branch_computations={%region_3.3_spmd, %region_4.4_spmd} | conditional | flops 16777228 | bytes 688299 | solution.py:59
  109.7 0.7 constant_dynamic-slice_fusion
  112.5 1.2 fusion
  114.6 4.7 %conditional.2 = (f32[128,1024]{1,0:T(8,128)S(1)}) conditional(s32[]{:T(128)} %bitcast.25, () %tuple.66, (s32[1,16]{1,0:T(1,128)S(1)}, s32[]{:T(128)}, s32[]{:T(128)}, bf16[1,8,128,128]{3,2,1,0:T(8,128)(2,1)}, s32[]{:T(128)}, /*index=5*/pred[]{:T(512)}, bf16[1024,1024]{1,0:T(8,128)(2,1)}) %tuple.67), branch_computations={%region_3.3_spmd, %region_4.4_spmd} | conditional | flops 16777228 | bytes 688299 | solution.py:59
  115.3 0.7 constant_dynamic-slice_fusion
  118.0 1.2 fusion
  120.1 0.8 conditional.2
  121.1 0.7 fusion.21
  121.8 0.8 conditional.2
  122.7 0.7 fusion.21
  123.4 0.8 conditional.2
  124.3 4.8 %all-reduce.4 = bf16[128,1024]{1,0:T(8,128)(2,1)S(1)} all-reduce(f32[128,1024]{1,0:T(8,128)S(1)} %bitcast.27), channel_id=1, replica_groups=mesh['rows'=16,'rep'=2] {'rep'}, use_global_device_ids=true, to_apply=%region_6.7 | all-reduce | flops 131072 | bytes 786432 | tf_op jit(solution)/shard_map/psum | solution.py:64
  129.2 2.6 %fusion.12 = (bf16[128,1024]{1,0:T(8,128)(2,1)}, f32[128,1024]{1,0:T(8,128)S(1)}) fusion(f32[128,1024]{1,0:T(8,128)} %fusion.13, bf16[128,1024]{1,0:T(8,128)(2,1)S(1)} %all-reduce.4, bf16[1024,1024]{1,0:T(8,128)(2,1)S(1)} %copy-done), kind=kOutput, calls=%fused_computation.21 | convolution fusion | flops 268697600 | bytes 3670016 | tf_op jit(solution)/shard_map/dot_general | solution.py:67
  131.7 0.9 fusion.7
  132.7 109.4 %all-reduce.3.cloned.1.call-done = f32[16,1024]{1,0:T(8,128)} async-done(((f32[16,1024]{1,0:T(8,128)}), f32[16,1024]{1,0:T(8,128)}) %all-reduce.3.cloned.1.call-update) | async-done | bytes 65552 | tf_op jit(solution)/shard_map/psum | solution.py:72
  242.1 1.5 copy.21
  (43 shorter events, 7.4 us)
Async XLA Ops:
  7.2 122.0 %copy-start = (bf16[1024,1024]{1,0:T(8,128)(2,1)S(1)}, bf16[1024,1024]{1,0:T(8,128)(2,1)}, u32[]{:S(2)}) copy-start(bf16[1024,1024]{1,0:T(8,128)(2,1)} %param.13) | copy-start | bytes 6291460
  7.2 67.3 %all-gather.2.cloned.1.call-start = ((), (), s32[]{:S(2)}) async-start(), calls=%async_computation | async-start | bytes 2228224 | tf_op jit(solution)/shard_map/all_gather | solution.py:33
  9.0 233.1 %all-reduce.3.cloned.1.call-start = ((), (), s32[]{:S(2)}) async-start(), calls=%async_computation.1 | async-start | bytes 131072 | tf_op jit(solution)/shard_map/psum | solution.py:72
  124.3 7.4 %copy-start.1 = (s32[128]{0:T(128)S(1)}, s32[128]{0:T(128)}, u32[]{:S(2)}) copy-start(s32[128]{0:T(128)} %param.17) | copy-start | bytes 1540
Sparse Core Ops, SparseCore 0:
  11.3 63.0 all-gather.1
  132.8 109.2 all-reduce.2
where the time goes:
time: 251 us; the launch traced here: 250 us
  waiting for transfers between devices  169 us (67%)
  loops' own time  25.4 us (10%)
  other arithmetic  14.8 us (6%)
  between operations  14.7 us (6%)
  matrix products  14 us (6%)
  local copies, waits for them, and re-layouts  7.68 us (3%)
  blocking collectives  4.82 us (2%)
    psum x1, waiting for transfers between devices, shards(): prompt_grad = lax.psum(prompt_part, 'rows')  109 us
    all_gather x1, waiting for transfers between devices, shards(): piece = lax.all_gather(mine, 'rows', axis=0, tiled=True)  59.5 us
    another operation x16, loops' own time, one_segment(): term = lax.cond(present[0, source], product, nothing, (block, rows_part))  24 us
    convert_element_type x16, other arithmetic, one_segment(): term = lax.cond(present[0, source], product, nothing, (block, rows_part))  10.6 us
    dot_general x6, matrix products, product(): return jnp.dot(blk, part_rows, preferred_element_type=jnp.float32)  7.16 us
  transfers between devices with their start and end apart: 2, of which 2 were waited for; matrix products, arithmetic and copies ran while one was open for 2% of the time, Pallas kernels for 0%

commit v1 on v0

v1 whole, which is shorter than its diff:
```python
import functools

import jax
import jax.numpy as jnp
from jax import lax
from jax.experimental import pallas as pl
from jax.experimental.pallas import tpu as pltpu
from jax.sharding import PartitionSpec as P

PROMPTS = 16
LANES = 128
CHUNKS = 2
MESH = pl.DeviceIdType.MESH
NT = (((1,), (1,)), ((), ()))
F32 = jnp.float32
BF16 = jnp.bfloat16


def split_rows(value):
    high = value.astype(BF16)
    low = (value - high.astype(F32)).astype(BF16)
    return jnp.concatenate([high, low], axis=0)


def kernel(
    na, nb, nrep,
    g_ref, ws_hbm, wn_hbm, adj_ref, index_ref, count_ref, ids_ref,
    out_ref, prompt_ref,
    ws, wn, gbuf, asend, arecv, ohsend, ohrecv, psend, precv, pown, agg, acc,
    pv, vsend, vrecv, usend, urecv, fin,
    w_sem, g_send, g_recv, a_send, a_recv, oh_send, oh_recv, p_send, p_recv,
    ag_send, ag_recv, v_send, v_recv, u_send, u_recv, f_send, f_recv,
):
    rows_dev, width = g_ref.shape
    slots = adj_ref.shape[1]
    half = width // nrep
    piece = half // CHUNKS
    group = nb * nrep
    vcols = width // group
    rows = lax.axis_index("rows")
    c = lax.axis_index("rep")
    a, b = rows // nb, rows % nb
    member = b * nrep + c

    load_ws = pltpu.make_async_copy(ws_hbm, ws, w_sem.at[0])
    load_wn = pltpu.make_async_copy(wn_hbm, wn, w_sem.at[1])
    load_ws.start()
    load_wn.start()

    def plane(k):
        return a * nb + (b + k) % nb

    def line(k):
        return (a + k) % na

    barrier = pltpu.get_barrier_semaphore()
    for k in range(1, na):
        pl.semaphore_signal(barrier, inc=1, device_id=(line(k) * nb + b, c), device_id_type=MESH)
    for k in range(1, group):
        other = (member + k) % group
        pl.semaphore_signal(
            barrier, inc=1, device_id=(a * nb + other // nrep, other % nrep), device_id_type=MESH
        )

    base = pl.multiple_of(c * half, half)

    def own_cols(q):
        return pl.ds(pl.multiple_of(base + q * piece, piece), piece)

    for q in range(CHUNKS):
        gbuf[q, pl.ds(pl.multiple_of(a * rows_dev, rows_dev), rows_dev), :] = g_ref[:, own_cols(q)]
    prompt_rows = lax.broadcasted_iota(jnp.int32, (PROMPTS, rows_dev), 0)
    onehot = jnp.where(ids_ref[...] == prompt_rows, 1.0, 0.0).astype(BF16)
    ohsend[...] = onehot
    ohrecv[b] = onehot
    pl.semaphore_wait(barrier, na - 1 + group - 1)

    def g_copy(q, source, step, own):
        place = pl.ds(pl.multiple_of(source * rows_dev, rows_dev), rows_dev)
        return pltpu.make_async_remote_copy(
            src_ref=g_ref.at[:, own_cols(q)] if own else gbuf.at[q, place, :],
            dst_ref=gbuf.at[q, place, :],
            send_sem=g_send.at[q, source, 0 if step > 0 else 1],
            recv_sem=g_recv.at[q, source],
            device_id=((a + step) * nb + b, c),
            device_id_type=MESH,
        )

    up, down = a + 1 < na, a >= 1
    for q in range(CHUNKS):
        @pl.when(up)
        def _():
            g_copy(q, a, 1, True).start()

        @pl.when(down)
        def _():
            g_copy(q, a, -1, True).start()

    def relay(d, q):
        @pl.when(a - d >= 0)
        def _():
            g_copy(q, a - d, 1, False).wait_recv()

            @pl.when(up)
            def _():
                g_copy(q, a - d, 1, False).start()

        @pl.when(a + d < na)
        def _():
            g_copy(q, a + d, -1, False).wait_recv()

            @pl.when(down)
            def _():
                g_copy(q, a + d, -1, False).start()

    def oh_copy(k):
        return pltpu.make_async_remote_copy(
            src_ref=ohsend, dst_ref=ohrecv.at[b], send_sem=oh_send.at[k], recv_sem=oh_recv.at[k],
            device_id=(plane(k), c), device_id_type=MESH,
        )

    def a_copy(k):
        return pltpu.make_async_remote_copy(
            src_ref=asend.at[k], dst_ref=arecv.at[b], send_sem=a_send.at[k], recv_sem=a_recv.at[k],
            device_id=(plane(k), c), device_id_type=MESH,
        )

    used = count_ref[0]

    def block_of(source):
        def look(k, found):
            slot, present = found
            hit = jnp.logical_and(index_ref[0, k] == source, k < used)
            return jnp.where(hit, k, slot), jnp.where(hit, 1.0, present)

        slot, present = lax.fori_loop(
            0, slots, look, (jnp.int32(0), jnp.float32(0.0)), unroll=slots <= 8
        )
        return (adj_ref[0, slot].astype(F32) * present).astype(BF16)

    def spread(ref, place, target):
        def one(j, carry):
            columns = pl.ds(pl.multiple_of(j * rows_dev, rows_dev), rows_dev)
            ref[place, :, columns] = block_of(j * nb + target)
            return carry

        lax.fori_loop(0, na, one, 0)

    for k in range(1, nb):
        oh_copy(k).start()
    for k in range(1, nb):
        spread(asend, k, (b + k) % nb)
        a_copy(k).start()
    spread(arecv, b, b)

    load_ws.wait()
    quarter = width // 4
    for d in range(1, na):
        for q in range(CHUNKS):
            relay(d, q)
        for part in range(4):
            if part * (na - 1) // 4 + 1 == d:
                columns = slice(part * quarter, (part + 1) * quarter)
                acc[:, columns] = lax.dot_general(
                    g_ref[...], ws[columns, :], NT, preferred_element_type=F32
                )

    def p_copy(q, k):
        return pltpu.make_async_remote_copy(
            src_ref=psend.at[q, k], dst_ref=precv.at[q, k],
            send_sem=p_send.at[q, k], recv_sem=p_recv.at[q, k],
            device_id=(plane(k), c), device_id_type=MESH,
        )

    for k in range(1, nb):
        oh_copy(k).wait_recv()
        a_copy(k).wait_recv()
    for q in range(CHUNKS):
        total = jnp.zeros((PROMPTS, piece), F32)
        for k in list(range(1, nb)) + [0]:
            target = (b + k) % nb
            part = jnp.dot(arecv[target], gbuf[q], preferred_element_type=F32)
            high = part.astype(BF16)
            if k:
                psend[q, k] = high
                p_copy(q, k).start()
            else:
                pown[q] = part
            low = (part - high.astype(F32)).astype(BF16)
            hot = ohrecv[target]
            total += jnp.dot(hot, high, preferred_element_type=F32)
            total += jnp.dot(hot, low, preferred_element_type=F32)
        pv[:, q * piece:(q + 1) * piece] = total

    load_wn.wait()
    own_half = pl.ds(base, half)
    own_sum = jnp.dot(ohsend[...], g_ref[:, own_half], preferred_element_type=F32)
    both = lax.dot_general(split_rows(own_sum), ws[:, own_half], NT, preferred_element_type=F32)
    both += lax.dot_general(split_rows(pv[...]), wn[:, own_half], NT, preferred_element_type=F32)
    value = both[:PROMPTS] + both[PROMPTS:]

    def member_id(m):
        return (a * nb + m // nrep, m % nrep)

    for m in range(group):
        vsend[m] = value[:, m * vcols:(m + 1) * vcols]

    def v_copy(k):
        m = (member + k) % group
        return pltpu.make_async_remote_copy(
            src_ref=vsend.at[m], dst_ref=vrecv.at[member], send_sem=v_send.at[k],
            recv_sem=v_recv.at[k], device_id=member_id(m), device_id_type=MESH,
        )

    for k in range(1, group):
        v_copy(k).start()
    vrecv[member] = vsend[member]

    def ag_copy(q, k):
        return pltpu.make_async_remote_copy(
            src_ref=agg.at[c, q], dst_ref=agg.at[c, q], send_sem=ag_send.at[q, k],
            recv_sem=ag_recv.at[q, k], device_id=(rows, (c + k) % nrep), device_id_type=MESH,
        )

    for q in range(CHUNKS):
        total = pown[q]
        for k in range(1, nb):
            p_copy(q, k).wait_recv()
            total += precv[q, k].astype(F32)
        agg[c, q] = total.astype(BF16)
        for k in range(1, nrep):
            ag_copy(q, k).start()

    for k in range(1, group):
        v_copy(k).wait_recv()
    total = vrecv[0]
    for m in range(1, group):
        total += vrecv[m]
    usend[...] = total
    urecv[a] = total

    def u_copy(k):
        return pltpu.make_async_remote_copy(
            src_ref=usend, dst_ref=urecv.at[a], send_sem=u_send.at[k], recv_sem=u_recv.at[k],
            device_id=(line(k) * nb + b, c), device_id_type=MESH,
        )

    for k in range(1, na):
        u_copy(k).start()

    def add_half(r):
        for q in range(CHUNKS):
            columns = pl.ds(pl.multiple_of(r * half + q * piece, piece), piece)
            acc[...] += lax.dot_general(
                agg[r, q], wn[:, columns], NT, preferred_element_type=F32
            )

    add_half(c)
    for k in range(1, nrep):
        for q in range(CHUNKS):
            ag_copy(q, k).wait_recv()
        add_half((c + nrep - k) % nrep)
    out_ref[...] = acc[...].astype(BF16)

    for k in range(1, na):
        u_copy(k).wait_recv()
    total = urecv[0]
    for m in range(1, na):
        total += urecv[m]
    usend2 = fin.at[member]
    fin[member] = total

    def f_copy(k):
        m = (member + k) % group
        return pltpu.make_async_remote_copy(
            src_ref=usend2, dst_ref=fin.at[member], send_sem=f_send.at[k], recv_sem=f_recv.at[k],
            device_id=member_id(m), device_id_type=MESH,
        )

    for k in range(1, group):
        f_copy(k).start()
    for k in range(1, group):
        f_copy(k).wait_recv()
    for m in range(group):
        prompt_ref[:, m * vcols:(m + 1) * vcols] = fin[m]

    for q in range(CHUNKS):
        @pl.when(up)
        def _():
            g_copy(q, a, 1, True).wait_send()

        @pl.when(down)
        def _():
            g_copy(q, a, -1, True).wait_send()

        for d in range(1, na):
            @pl.when(jnp.logical_and(a - d >= 0, up))
            def _():
                g_copy(q, a - d, 1, False).wait_send()

            @pl.when(jnp.logical_and(a + d < na, down))
            def _():
                g_copy(q, a + d, -1, False).wait_send()

        for k in range(1, nb):
            p_copy(q, k).wait_send()
        for k in range(1, nrep):
            ag_copy(q, k).wait_send()
    for k in range(1, nb):
        oh_copy(k).wait_send()
        a_copy(k).wait_send()
    for k in range(1, na):
        u_copy(k).wait_send()
    for k in range(1, group):
        v_copy(k).wait_send()
        f_copy(k).wait_send()


def solution(mesh):
    n, nrep = mesh.shape["rows"], mesh.shape["rep"]

    def shards(grad_out, w_self, w_neigh, adj_tiles, tile_index, tile_count, prompt_ids):
        rows_dev, width = grad_out.shape
        nb = 1
        while n % (2 * nb) == 0 and 4 * nb * nb <= n and width % (2 * nb * nrep * LANES) == 0:
            nb *= 2
        na = n // nb
        half = width // nrep
        piece = half // CHUNKS
        group = nb * nrep
        vcols = width // group
        vmem = pl.BlockSpec(memory_space=pltpu.VMEM)
        smem = pl.BlockSpec(memory_space=pltpu.SMEM)
        hbm = pl.BlockSpec(memory_space=pl.ANY)
        dma = pltpu.SemaphoreType.DMA
        return pl.pallas_call(
            functools.partial(kernel, na, nb, nrep),
            out_shape=(
                jax.ShapeDtypeStruct((rows_dev, width), BF16),
                jax.ShapeDtypeStruct((PROMPTS, width), F32),
            ),
            in_specs=[vmem, hbm, hbm, vmem, smem, smem, vmem],
            out_specs=(vmem, vmem),
            scratch_shapes=[
                pltpu.VMEM((width, width), BF16),
                pltpu.VMEM((width, width), BF16),
                pltpu.VMEM((CHUNKS, na * rows_dev, piece), BF16),
                pltpu.VMEM((nb, rows_dev, na * rows_dev), BF16),
                pltpu.VMEM((nb, rows_dev, na * rows_dev), BF16),
                pltpu.VMEM((PROMPTS, rows_dev), BF16),
                pltpu.VMEM((nb, PROMPTS, rows_dev), BF16),
                pltpu.VMEM((CHUNKS, nb, rows_dev, piece), BF16),
                pltpu.VMEM((CHUNKS, nb, rows_dev, piece), BF16),
                pltpu.VMEM((CHUNKS, rows_dev, piece), F32),
                pltpu.VMEM((nrep, CHUNKS, rows_dev, piece), BF16),
                pltpu.VMEM((rows_dev, width), F32),
                pltpu.VMEM((PROMPTS, half), F32),
                pltpu.VMEM((group, PROMPTS, vcols), F32),
                pltpu.VMEM((group, PROMPTS, vcols), F32),
                pltpu.VMEM((PROMPTS, vcols), F32),
                pltpu.VMEM((na, PROMPTS, vcols), F32),
                pltpu.VMEM((group, PROMPTS, vcols), F32),
                dma((2,)),
                dma((CHUNKS, na, 2)),
                dma((CHUNKS, na)),
                dma((nb,)),
                dma((nb,)),
                dma((nb,)),
                dma((nb,)),
                dma((CHUNKS, nb)),
                dma((CHUNKS, nb)),
                dma((CHUNKS, nrep)),
                dma((CHUNKS, nrep)),
                dma((group,)),
                dma((group,)),
                dma((na,)),
                dma((na,)),
                dma((group,)),
                dma((group,)),
            ],
            compiler_params=pltpu.CompilerParams(
                collective_id=0, has_side_effects=True, vmem_limit_bytes=60 * 2 ** 20
            ),
        )(
            grad_out, w_self, w_neigh, adj_tiles, tile_index, tile_count,
            prompt_ids.reshape(1, rows_dev),
        )

    placed = (
        P("rows", None),
        P(),
        P(),
        P("rows", None, None, None),
        P("rows", None),
        P("rows"),
        P("rows"),
    )
    return jax.shard_map(
        shards, mesh=mesh, in_specs=placed, out_specs=(P("rows", None), P()), check_vma=False
    )
```

time: 251 us -> 37.4 us (0.15)
  waiting for transfers between devices: 169 us -> 0 us
  Pallas kernels: 0 us -> 32.7 us
  loops' own time: 25.4 us -> 0 us
  other arithmetic: 14.8 us -> 0 us
  matrix products: 14 us -> 0 us
  between operations: 14.7 us -> 1.29 us
  blocking collectives: 4.82 us -> 0 us
  local copies, waits for them, and re-layouts: 7.68 us -> 3.14 us
    psum x1 -> x0, waiting for transfers between devices: 109 us -> none  [shards(): prompt_grad = lax.psum(prompt_part, 'rows')]
    all_gather x1 -> x0, waiting for transfers between devices: 59.5 us -> none  [shards(): piece = lax.all_gather(mine, 'rows', axis=0, tiled=True)]
    pallas_call x0 -> x1, Pallas kernels: none -> 32.7 us  [shards(): pl.pallas_call(functools.partial(kernel, na, nb, nrep), out_shape=(jax.Sh...]
    another operation x17 -> x0, loops' own time: 25.4 us -> none  [the longest x16 24 us: one_segment(): term = lax.cond(present[0, source], product, nothing, (block, rows_part))]
    dot_general x9 -> x0, matrix products: 14 us -> none  [the longest x6 7.16 us: product(): return jnp.dot(blk, part_rows, preferred_element_type=jnp.float32)]
    convert_element_type x16 -> x0, other arithmetic: 10.6 us -> none  [one_segment(): term = lax.cond(present[0, source], product, nothing, (block, rows_part))]
    dynamic_slice x7 -> x0, local copies, waits for them, and re-layouts: 5.71 us -> none  [the longest x6 4 us: one_segment(): slot = slot_table[0, source]]
    psum x1 -> x0, blocking collectives: 4.82 us -> none  [shards(): summed = lax.psum(partial_value.reshape(rows_dev, width), 'rep')]
  transfers between devices with their start and end apart: 2 -> 0, of which waited for: 2 -> 0; matrix products, arithmetic and copies ran while one was open for 2% -> 0% of each run, Pallas kernels for 0% -> 0%
where the time goes in v1:
time: 37.4 us; the launch traced here: 37.1 us
  Pallas kernels  32.7 us (87%)
  local copies, waits for them, and re-layouts  3.14 us (8%)
  between operations  1.29 us (3%)
    pallas_call x1, Pallas kernels, shards(): pl.pallas_call(functools.partial(kernel, na, nb, nrep), out_shape=(jax.Sh...  32.7 us
    unnamed x2, local copies, waits for them, and re-layouts  3.14 us

profile of v1, /device:TPU:0, one launch (start us, length us, event | category | flops | bytes accessed | tf_op | source)
XLA Modules:
  0.0 37.1 jit_solution(8918917963258739721)
XLA Ops:
  1.3 32.7 %shard_map.86 = (bf16[128,1024]{1,0:T(8,128)(2,1)}, f32[16,1024]{1,0:T(8,128)}) custom-call(bf16[128,1024]{1,0:T(8,128)(2,1)} %g_ref.1, bf16[1024,1024]{1,0:T(8,128)(2,1)} %ws_hbm.1, bf16[1024,1024]{1,0:T(8,128)(2,1)} %wn_hbm.1, bf16[1,8,128,128]{3,2,1,0:T(8,128)(2,1)} %adj_ref.1, s32[1,8]{1,0:T(1,128)} %index_ref.1, s32[1]{0:T(128)S(6)} %copy.11.count_ref, ...), custom_call_target="tpu_custom_call" | custom-call | tf_op jit(solution)/shard_map/pallas_call | solution.py:336
  34.0 1.7 %copy.12 = bf16[128,1024]{1,0:T(8,128)(2,1)} copy(bf16[128,1024]{1,0:T(8,128)(2,1)} %get-tuple-element.4) | data formatting | bytes 524288
  35.7 1.5 %copy.13 = f32[16,1024]{1,0:T(8,128)} copy(f32[16,1024]{1,0:T(8,128)} %get-tuple-element.5) | data formatting | bytes 131072

commit v2 on v1

--- a/solution.py
+++ b/solution.py
@@ -9,7 +9,7 @@
 
 PROMPTS = 16
 LANES = 128
-CHUNKS = 2
+CHUNKS = 4
 MESH = pl.DeviceIdType.MESH
 NT = (((1,), (1,)), ((), ()))
 F32 = jnp.float32
@@ -24,15 +24,16 @@
 
 def kernel(
     na, nb, nrep,
-    g_ref, ws_hbm, wn_hbm, adj_ref, index_ref, count_ref, ids_ref,
+    g_hbm, ws_hbm, wn_hbm, adj_hbm, index_ref, count_ref, ids_ref,
     out_ref, prompt_ref,
-    ws, wn, gbuf, asend, arecv, ohsend, ohrecv, psend, precv, pown, agg, acc,
-    pv, vsend, vrecv, usend, urecv, fin,
-    w_sem, g_send, g_recv, a_send, a_recv, oh_send, oh_recv, p_send, p_recv,
+    g_ref, adj_ref, ws, wn, gbuf, asend, arecv, ohsend, ohrecv, psend, precv, pown, agg, acc,
+    pv, vself, vsend, vrecv, usend, urecv, fin,
+    w_sem, g_send, g_recv, a_send, a_recv, fa_send, fa_recv, oh_send, oh_recv, p_send, p_recv,
     ag_send, ag_recv, v_send, v_recv, u_send, u_recv, f_send, f_recv,
 ):
     rows_dev, width = g_ref.shape
     slots = adj_ref.shape[1]
+    share = rows_dev // nrep
     half = width // nrep
     piece = half // CHUNKS
     group = nb * nrep
@@ -44,6 +45,10 @@
 
     load_ws = pltpu.make_async_copy(ws_hbm, ws, w_sem.at[0])
     load_wn = pltpu.make_async_copy(wn_hbm, wn, w_sem.at[1])
+    load_g = pltpu.make_async_copy(g_hbm, g_ref, w_sem.at[2])
+    load_adj = pltpu.make_async_copy(adj_hbm, adj_ref, w_sem.at[3])
+    load_g.start()
+    load_adj.start()
     load_ws.start()
     load_wn.start()
 
@@ -67,12 +72,11 @@
     def own_cols(q):
         return pl.ds(pl.multiple_of(base + q * piece, piece), piece)
 
-    for q in range(CHUNKS):
-        gbuf[q, pl.ds(pl.multiple_of(a * rows_dev, rows_dev), rows_dev), :] = g_ref[:, own_cols(q)]
     prompt_rows = lax.broadcasted_iota(jnp.int32, (PROMPTS, rows_dev), 0)
     onehot = jnp.where(ids_ref[...] == prompt_rows, 1.0, 0.0).astype(BF16)
     ohsend[...] = onehot
     ohrecv[b] = onehot
+    load_g.wait()
     pl.semaphore_wait(barrier, na - 1 + group - 1)
 
     def g_copy(q, source, step, own):
@@ -87,7 +91,8 @@
         )
 
     up, down = a + 1 < na, a >= 1
-    for q in range(CHUNKS):
+
+    def send_own(q):
         @pl.when(up)
         def _():
             g_copy(q, a, 1, True).start()
@@ -95,6 +100,9 @@
         @pl.when(down)
         def _():
             g_copy(q, a, -1, True).start()
+
+    send_own(0)
+    send_own(1)
 
     def relay(d, q):
         @pl.when(a - d >= 0)
@@ -119,15 +127,25 @@
             device_id=(plane(k), c), device_id_type=MESH,
         )
 
+    my_share = pl.ds(pl.multiple_of(c * share, share), share)
+
     def a_copy(k):
         return pltpu.make_async_remote_copy(
-            src_ref=asend.at[k], dst_ref=arecv.at[b], send_sem=a_send.at[k], recv_sem=a_recv.at[k],
+            src_ref=asend.at[k], dst_ref=arecv.at[b, my_share, :], send_sem=a_send.at[k], recv_sem=a_recv.at[k],
             device_id=(plane(k), c), device_id_type=MESH,
         )
 
-    used = count_ref[0]
-
-    def block_of(source):
+    def fa_copy(k, r):
+        source = (b + nb - k) % nb
+        return pltpu.make_async_remote_copy(
+            src_ref=arecv.at[source, my_share, :], dst_ref=arecv.at[source, my_share, :],
+            send_sem=fa_send.at[k, r], recv_sem=fa_recv.at[k, r],
+            device_id=(rows, (c + r) % nrep), device_id_type=MESH,
+        )
+
+    used = count_ref[0, 0]
+
+    def block_of(source, part):
         def look(k, found):
             slot, present = found
             hit = jnp.logical_and(index_ref[0, k] == source, k < used)
@@ -136,34 +154,44 @@
         slot, present = lax.fori_loop(
             0, slots, look, (jnp.int32(0), jnp.float32(0.0)), unroll=slots <= 8
         )
-        return (adj_ref[0, slot].astype(F32) * present).astype(BF16)
-
-    def spread(ref, place, target):
+        return (adj_ref[0, slot, part, :].astype(F32) * present).astype(BF16)
+
+    def spread(ref, place, target, part):
         def one(j, carry):
             columns = pl.ds(pl.multiple_of(j * rows_dev, rows_dev), rows_dev)
-            ref[place, :, columns] = block_of(j * nb + target)
+            ref[place, :, columns] = block_of(j * nb + target, part)
             return carry
 
         lax.fori_loop(0, na, one, 0)
 
     for k in range(1, nb):
         oh_copy(k).start()
+    load_adj.wait()
     for k in range(1, nb):
-        spread(asend, k, (b + k) % nb)
+        spread(asend, k, (b + k) % nb, my_share)
         a_copy(k).start()
-    spread(arecv, b, b)
-
+    spread(arecv, b, b, slice(None))
+    for q in range(CHUNKS):
+        gbuf[q, pl.ds(pl.multiple_of(a * rows_dev, rows_dev), rows_dev), :] = g_ref[:, own_cols(q)]
     load_ws.wait()
+    load_wn.wait()
+    own_half = pl.ds(base, half)
     quarter = width // 4
-    for d in range(1, na):
-        for q in range(CHUNKS):
-            relay(d, q)
-        for part in range(4):
-            if part * (na - 1) // 4 + 1 == d:
-                columns = slice(part * quarter, (part + 1) * quarter)
-                acc[:, columns] = lax.dot_general(
-                    g_ref[...], ws[columns, :], NT, preferred_element_type=F32
-                )
+
+    def self_part(part):
+        columns = slice(part * quarter, (part + 1) * quarter)
+        acc[:, columns] = lax.dot_general(
+            g_ref[...], ws[columns, :], NT, preferred_element_type=F32
+        )
+
+    def fold(value):
+        return value[:PROMPTS] + value[PROMPTS:]
+
+    def self_prompts():
+        own_sum = jnp.dot(ohsend[...], g_ref[:, own_half], preferred_element_type=F32)
+        vself[...] = fold(lax.dot_general(
+            split_rows(own_sum), ws[:, own_half], NT, preferred_element_type=F32
+        ))
 
     def p_copy(q, k):
         return pltpu.make_async_remote_copy(
@@ -172,10 +200,7 @@
             device_id=(plane(k), c), device_id_type=MESH,
         )
 
-    for k in range(1, nb):
-        oh_copy(k).wait_recv()
-        a_copy(k).wait_recv()
-    for q in range(CHUNKS):
+    def partials(q):
         total = jnp.zeros((PROMPTS, piece), F32)
         for k in list(range(1, nb)) + [0]:
             target = (b + k) % nb
@@ -183,7 +208,8 @@
             high = part.astype(BF16)
             if k:
                 psend[q, k] = high
-                p_copy(q, k).start()
+                if q < CHUNKS - 1:
+                    p_copy(q, k).start()
             else:
                 pown[q] = part
             low = (part - high.astype(F32)).astype(BF16)
@@ -192,12 +218,32 @@
             total += jnp.dot(hot, low, preferred_element_type=F32)
         pv[:, q * piece:(q + 1) * piece] = total
 
-    load_wn.wait()
-    own_half = pl.ds(base, half)
-    own_sum = jnp.dot(ohsend[...], g_ref[:, own_half], preferred_element_type=F32)
-    both = lax.dot_general(split_rows(own_sum), ws[:, own_half], NT, preferred_element_type=F32)
-    both += lax.dot_general(split_rows(pv[...]), wn[:, own_half], NT, preferred_element_type=F32)
-    value = both[:PROMPTS] + both[PROMPTS:]
+    for t in range(CHUNKS + na - 1):
+        if 2 <= t + 1 < CHUNKS:
+            send_own(t + 1)
+        for d in range(1, na):
+            if 0 <= t - d < CHUNKS:
+                relay(d, t - d)
+        if t == na - 2:
+            for k in range(1, nb):
+                a_copy(k).wait_recv()
+                for r in range(1, nrep):
+                    fa_copy(k, r).start()
+        for part in range(4):
+            if part * (na - 1) // 4 == t:
+                self_part(part)
+        if t == na - 1:
+            self_prompts()
+            for k in range(1, nb):
+                oh_copy(k).wait_recv()
+                for r in range(1, nrep):
+                    fa_copy(k, r).wait_recv()
+        if t >= na - 1:
+            partials(t - na + 1)
+
+    value = vself[...] + fold(lax.dot_general(
+        split_rows(pv[...]), wn[:, own_half], NT, preferred_element_type=F32
+    ))
 
     def member_id(m):
         return (a * nb + m // nrep, m % nrep)
@@ -214,6 +260,8 @@
 
     for k in range(1, group):
         v_copy(k).start()
+    for k in range(1, nb):
+        p_copy(CHUNKS - 1, k).start()
     vrecv[member] = vsend[member]
 
     def ag_copy(q, k):
@@ -249,11 +297,9 @@
         u_copy(k).start()
 
     def add_half(r):
-        for q in range(CHUNKS):
-            columns = pl.ds(pl.multiple_of(r * half + q * piece, piece), piece)
-            acc[...] += lax.dot_general(
-                agg[r, q], wn[:, columns], NT, preferred_element_type=F32
-            )
+        columns = pl.ds(pl.multiple_of(r * half, half), half)
+        joined = jnp.concatenate([agg[r, q] for q in range(CHUNKS)], axis=1)
+        acc[...] += lax.dot_general(joined, wn[:, columns], NT, preferred_element_type=F32)
 
     add_half(c)
     for k in range(1, nrep):
@@ -309,11 +355,24 @@
     for k in range(1, nb):
         oh_copy(k).wait_send()
         a_copy(k).wait_send()
+        for r in range(1, nrep):
+            fa_copy(k, r).wait_send()
     for k in range(1, na):
         u_copy(k).wait_send()
     for k in range(1, group):
         v_copy(k).wait_send()
         f_copy(k).wait_send()
+
+
+def put_out(held_out, held_prompt, out_hbm, prompt_hbm, sem):
+    copies = [
+        pltpu.make_async_copy(held_out, out_hbm, sem.at[0]),
+        pltpu.make_async_copy(held_prompt, prompt_hbm, sem.at[1]),
+    ]
+    for copy in copies:
+        copy.start()
+    for copy in copies:
+        copy.wait()
 
 
 def solution(mesh):
@@ -333,19 +392,21 @@
         smem = pl.BlockSpec(memory_space=pltpu.SMEM)
         hbm = pl.BlockSpec(memory_space=pl.ANY)
         dma = pltpu.SemaphoreType.DMA
-        return pl.pallas_call(
+        held = pl.pallas_call(
             functools.partial(kernel, na, nb, nrep),
             out_shape=(
-                jax.ShapeDtypeStruct((rows_dev, width), BF16),
-                jax.ShapeDtypeStruct((PROMPTS, width), F32),
+                pltpu.VMEM((rows_dev, width), BF16),
+                pltpu.VMEM((PROMPTS, width), F32),
             ),
-            in_specs=[vmem, hbm, hbm, vmem, smem, smem, vmem],
+            in_specs=[hbm, hbm, hbm, hbm, smem, smem, vmem],
             out_specs=(vmem, vmem),
             scratch_shapes=[
+                pltpu.VMEM((rows_dev, width), BF16),
+                pltpu.VMEM(adj_tiles.shape, BF16),
                 pltpu.VMEM((width, width), BF16),
                 pltpu.VMEM((width, width), BF16),
                 pltpu.VMEM((CHUNKS, na * rows_dev, piece), BF16),
-                pltpu.VMEM((nb, rows_dev, na * rows_dev), BF16),
+                pltpu.VMEM((nb, rows_dev // nrep, na * rows_dev), BF16),
                 pltpu.VMEM((nb, rows_dev, na * rows_dev), BF16),
                 pltpu.VMEM((PROMPTS, rows_dev), BF16),
                 pltpu.VMEM((nb, PROMPTS, rows_dev), BF16),
@@ -355,16 +416,19 @@
                 pltpu.VMEM((nrep, CHUNKS, rows_dev, piece), BF16),
                 pltpu.VMEM((rows_dev, width), F32),
                 pltpu.VMEM((PROMPTS, half), F32),
+                pltpu.VMEM((PROMPTS, width), F32),
                 pltpu.VMEM((group, PROMPTS, vcols), F32),
                 pltpu.VMEM((group, PROMPTS, vcols), F32),
                 pltpu.VMEM((PROMPTS, vcols), F32),
                 pltpu.VMEM((na, PROMPTS, vcols), F32),
                 pltpu.VMEM((group, PROMPTS, vcols), F32),
-                dma((2,)),
+                dma((4,)),
                 dma((CHUNKS, na, 2)),
                 dma((CHUNKS, na)),
                 dma((nb,)),
                 dma((nb,)),
+                dma((nb, nrep)),
+                dma((nb, nrep)),
                 dma((nb,)),
                 dma((nb,)),
                 dma((CHUNKS, nb)),
@@ -379,12 +443,23 @@
                 dma((group,)),
             ],
             compiler_params=pltpu.CompilerParams(
-                collective_id=0, has_side_effects=True, vmem_limit_bytes=60 * 2 ** 20
+                collective_id=0, has_side_effects=True, vmem_limit_bytes=56 * 2 ** 20
             ),
         )(
-            grad_out, w_self, w_neigh, adj_tiles, tile_index, tile_count,
+            grad_out, w_self, w_neigh, adj_tiles, tile_index, tile_count.reshape(1, 1),
             prompt_ids.reshape(1, rows_dev),
         )
+        return pl.pallas_call(
+            put_out,
+            out_shape=(
+                jax.ShapeDtypeStruct((rows_dev, width), BF16),
+                jax.ShapeDtypeStruct((PROMPTS, width), F32),
+            ),
+            in_specs=[vmem, vmem],
+            out_specs=(hbm, hbm),
+            scratch_shapes=[dma((2,))],
+            compiler_params=pltpu.CompilerParams(vmem_limit_bytes=2 ** 20),
+        )(*held)
 
     placed = (
         P("rows", None),

time: 37.4 us -> 36.2 us (0.968)
  local copies, waits for them, and re-layouts: 3.14 us -> 0 us
  Pallas kernels: 32.7 us -> 34.8 us
    unnamed x2 -> x0, local copies, waits for them, and re-layouts: 3.14 us -> none
    pallas_call x1 -> x2, Pallas kernels: 32.7 us -> 34.8 us  [the longest x1 34.1 us: shards(): pl.pallas_call(functools.partial(kernel, na, nb, nrep), out_shape=(pltpu....]
where the time goes in v2:
time: 36.2 us; the launch traced here: 36.1 us
  Pallas kernels  34.8 us (96%)
  between operations  1.29 us (4%)
    pallas_call x1, Pallas kernels, shards(): pl.pallas_call(functools.partial(kernel, na, nb, nrep), out_shape=(pltpu....  34.1 us
    pallas_call x1, Pallas kernels, shards(): pl.pallas_call(put_out, out_shape=(jax.ShapeDtypeStruct((rows_dev, width)...  0.74 us

profile of v2, /device:TPU:0, one launch (start us, length us, event | category | flops | bytes accessed | tf_op | source)
XLA Modules:
  0.0 36.1 jit_solution(3030184100836013829)
XLA Ops:
  1.3 34.1 %shard_map.86 = (bf16[128,1024]{1,0:T(8,128)(2,1)S(1)}, f32[16,1024]{1,0:T(8,128)S(1)}) custom-call(bf16[128,1024]{1,0:T(8,128)(2,1)} %g_hbm.1, bf16[1024,1024]{1,0:T(8,128)(2,1)} %ws_hbm.1, bf16[1024,1024]{1,0:T(8,128)(2,1)} %wn_hbm.1, bf16[1,8,128,128]{3,2,1,0:T(8,128)(2,1)} %adj_hbm.1, s32[1,8]{1,0:T(1,128)} %index_ref.1, s32[1,1]{1,0:T(1,128)} %bitcast.2.count_ref, ...), custom_call_target="tpu_custom_call" | custom-call | tf_op jit(solution)/shard_map/pallas_call | solution.py:395
  35.3 0.7 %shard_map.87 = (bf16[128,1024]{1,0:T(8,128)(2,1)}, f32[16,1024]{1,0:T(8,128)}) custom-call(bf16[128,1024]{1,0:T(8,128)(2,1)S(1)} %get-tuple-element.4.held_out, f32[16,1024]{1,0:T(8,128)S(1)} %get-tuple-element.5.held_prompt), custom_call_target="tpu_custom_call" | custom-call | tf_op jit(solution)/shard_map/pallas_call | solution.py:452

commit v3 on v2

--- a/solution.py
+++ b/solution.py
@@ -27,9 +27,9 @@
     g_hbm, ws_hbm, wn_hbm, adj_hbm, index_ref, count_ref, ids_ref,
     out_ref, prompt_ref,
     g_ref, adj_ref, ws, wn, gbuf, asend, arecv, ohsend, ohrecv, psend, precv, pown, agg, acc,
-    pv, vself, vsend, vrecv, usend, urecv, fin,
+    csend, crecv, vself, vsend, vrecv, usend, urecv, fin,
     w_sem, g_send, g_recv, a_send, a_recv, fa_send, fa_recv, oh_send, oh_recv, p_send, p_recv,
-    ag_send, ag_recv, v_send, v_recv, u_send, u_recv, f_send, f_recv,
+    ag_send, ag_recv, c_send, c_recv, v_send, v_recv, u_send, u_recv, f_send, f_recv,
 ):
     rows_dev, width = g_ref.shape
     slots = adj_ref.shape[1]
@@ -101,8 +101,8 @@
         def _():
             g_copy(q, a, -1, True).start()
 
-    send_own(0)
-    send_own(1)
+    for q in range(CHUNKS):
+        send_own(q)
 
     def relay(d, q):
         @pl.when(a - d >= 0)
@@ -201,26 +201,57 @@
         )
 
     def partials(q):
-        total = jnp.zeros((PROMPTS, piece), F32)
         for k in list(range(1, nb)) + [0]:
-            target = (b + k) % nb
-            part = jnp.dot(arecv[target], gbuf[q], preferred_element_type=F32)
-            high = part.astype(BF16)
+            part = jnp.dot(arecv[(b + k) % nb], gbuf[q], preferred_element_type=F32)
             if k:
-                psend[q, k] = high
-                if q < CHUNKS - 1:
-                    p_copy(q, k).start()
+                psend[q, k] = part.astype(BF16)
+                p_copy(q, k).start()
             else:
                 pown[q] = part
-            low = (part - high.astype(F32)).astype(BF16)
-            hot = ohrecv[target]
-            total += jnp.dot(hot, high, preferred_element_type=F32)
-            total += jnp.dot(hot, low, preferred_element_type=F32)
-        pv[:, q * piece:(q + 1) * piece] = total
+
+    def c_copy(k):
+        return pltpu.make_async_remote_copy(
+            src_ref=csend.at[line(k)], dst_ref=crecv.at[a], send_sem=c_send.at[k],
+            recv_sem=c_recv.at[k], device_id=(line(k) * nb + b, c), device_id_type=MESH,
+        )
+
+    def send_coefficients():
+        total = jnp.zeros((PROMPTS, na * rows_dev), F32)
+        for k in range(nb):
+            total += jnp.dot(ohrecv[k], arecv[k], preferred_element_type=F32)
+        for m in range(na):
+            csend[m] = total[:, m * rows_dev:(m + 1) * rows_dev]
+        for k in range(1, na):
+            c_copy(k).start()
+        crecv[a] = csend[a]
+
+    def member_id(m):
+        return (a * nb + m // nrep, m % nrep)
+
+    def v_copy(k):
+        m = (member + k) % group
+        return pltpu.make_async_remote_copy(
+            src_ref=vsend.at[m], dst_ref=vrecv.at[member], send_sem=v_send.at[k],
+            recv_sem=v_recv.at[k], device_id=member_id(m), device_id_type=MESH,
+        )
+
+    def send_prompts():
+        for k in range(1, na):
+            c_copy(k).wait_recv()
+        total = crecv[0]
+        for m in range(1, na):
+            total += crecv[m]
+        through = fold(jnp.dot(split_rows(total), g_ref[:, own_half], preferred_element_type=F32))
+        value = vself[...] + fold(lax.dot_general(
+            split_rows(through), wn[:, own_half], NT, preferred_element_type=F32
+        ))
+        for m in range(group):
+            vsend[m] = value[:, m * vcols:(m + 1) * vcols]
+        for k in range(1, group):
+            v_copy(k).start()
+        vrecv[member] = vsend[member]
 
     for t in range(CHUNKS + na - 1):
-        if 2 <= t + 1 < CHUNKS:
-            send_own(t + 1)
         for d in range(1, na):
             if 0 <= t - d < CHUNKS:
                 relay(d, t - d)
@@ -238,37 +269,34 @@
                 oh_copy(k).wait_recv()
                 for r in range(1, nrep):
                     fa_copy(k, r).wait_recv()
+            send_coefficients()
         if t >= na - 1:
             partials(t - na + 1)
-
-    value = vself[...] + fold(lax.dot_general(
-        split_rows(pv[...]), wn[:, own_half], NT, preferred_element_type=F32
-    ))
-
-    def member_id(m):
-        return (a * nb + m // nrep, m % nrep)
-
-    for m in range(group):
-        vsend[m] = value[:, m * vcols:(m + 1) * vcols]
-
-    def v_copy(k):
-        m = (member + k) % group
-        return pltpu.make_async_remote_copy(
-            src_ref=vsend.at[m], dst_ref=vrecv.at[member], send_sem=v_send.at[k],
-            recv_sem=v_recv.at[k], device_id=member_id(m), device_id_type=MESH,
-        )
-
-    for k in range(1, group):
-        v_copy(k).start()
-    for k in range(1, nb):
-        p_copy(CHUNKS - 1, k).start()
-    vrecv[member] = vsend[member]
+        if t == CHUNKS + na - 3:
+            send_prompts()
 
     def ag_copy(q, k):
         return pltpu.make_async_remote_copy(
             src_ref=agg.at[c, q], dst_ref=agg.at[c, q], send_sem=ag_send.at[q, k],
             recv_sem=ag_recv.at[q, k], device_id=(rows, (c + k) % nrep), device_id_type=MESH,
         )
+
+    for k in range(1, group):
+        v_copy(k).wait_recv()
+    total = vrecv[0]
+    for m in range(1, group):
+        total += vrecv[m]
+    usend[...] = total
+    urecv[a] = total
+
+    def u_copy(k):
+        return pltpu.make_async_remote_copy(
+            src_ref=usend, dst_ref=urecv.at[a], send_sem=u_send.at[k], recv_sem=u_recv.at[k],
+            device_id=(line(k) * nb + b, c), device_id_type=MESH,
+        )
+
+    for k in range(1, na):
+        u_copy(k).start()
 
     for q in range(CHUNKS):
         total = pown[q]
@@ -279,35 +307,12 @@
         for k in range(1, nrep):
             ag_copy(q, k).start()
 
-    for k in range(1, group):
-        v_copy(k).wait_recv()
-    total = vrecv[0]
-    for m in range(1, group):
-        total += vrecv[m]
-    usend[...] = total
-    urecv[a] = total
-
-    def u_copy(k):
-        return pltpu.make_async_remote_copy(
-            src_ref=usend, dst_ref=urecv.at[a], send_sem=u_send.at[k], recv_sem=u_recv.at[k],
-            device_id=(line(k) * nb + b, c), device_id_type=MESH,
-        )
-
-    for k in range(1, na):
-        u_copy(k).start()
-
     def add_half(r):
         columns = pl.ds(pl.multiple_of(r * half, half), half)
         joined = jnp.concatenate([agg[r, q] for q in range(CHUNKS)], axis=1)
         acc[...] += lax.dot_general(joined, wn[:, columns], NT, preferred_element_type=F32)
 
     add_half(c)
-    for k in range(1, nrep):
-        for q in range(CHUNKS):
-            ag_copy(q, k).wait_recv()
-        add_half((c + nrep - k) % nrep)
-    out_ref[...] = acc[...].astype(BF16)
-
     for k in range(1, na):
         u_copy(k).wait_recv()
     total = urecv[0]
@@ -325,6 +330,12 @@
 
     for k in range(1, group):
         f_copy(k).start()
+    for k in range(1, nrep):
+        for q in range(CHUNKS):
+            ag_copy(q, k).wait_recv()
+        add_half((c + nrep - k) % nrep)
+    out_ref[...] = acc[...].astype(BF16)
+
     for k in range(1, group):
         f_copy(k).wait_recv()
     for m in range(group):
@@ -358,6 +369,7 @@
         for r in range(1, nrep):
             fa_copy(k, r).wait_send()
     for k in range(1, na):
+        c_copy(k).wait_send()
         u_copy(k).wait_send()
     for k in range(1, group):
         v_copy(k).wait_send()
@@ -415,7 +427,8 @@
                 pltpu.VMEM((CHUNKS, rows_dev, piece), F32),
                 pltpu.VMEM((nrep, CHUNKS, rows_dev, piece), BF16),
                 pltpu.VMEM((rows_dev, width), F32),
-                pltpu.VMEM((PROMPTS, half), F32),
+                pltpu.VMEM((na, PROMPTS, rows_dev), F32),
+                pltpu.VMEM((na, PROMPTS, rows_dev), F32),
                 pltpu.VMEM((PROMPTS, width), F32),
                 pltpu.VMEM((group, PROMPTS, vcols), F32),
                 pltpu.VMEM((group, PROMPTS, vcols), F32),
@@ -435,6 +448,8 @@
                 dma((CHUNKS, nb)),
                 dma((CHUNKS, nrep)),
                 dma((CHUNKS, nrep)),
+                dma((na,)),
+                dma((na,)),
                 dma((group,)),
                 dma((group,)),
                 dma((na,)),

time: 36.2 us -> 34.1 us (0.942)
  Pallas kernels: 34.8 us -> 32.6 us
    pallas_call x1, Pallas kernels: 34.1 us -> 31.9 us  [shards(): pl.pallas_call(functools.partial(kernel, na, nb, nrep), out_shape=(pltpu....]
where the time goes in v3:
time: 34.1 us; the launch traced here: 33.9 us
  Pallas kernels  32.6 us (96%)
  between operations  1.29 us (4%)
    pallas_call x1, Pallas kernels, shards(): pl.pallas_call(functools.partial(kernel, na, nb, nrep), out_shape=(pltpu....  31.9 us
    pallas_call x1, Pallas kernels, shards(): pl.pallas_call(put_out, out_shape=(jax.ShapeDtypeStruct((rows_dev, width)...  0.74 us

profile of v3, /device:TPU:0, one launch (start us, length us, event | category | flops | bytes accessed | tf_op | source)
XLA Modules:
  0.0 33.9 jit_solution(3021246177354047977)
XLA Ops:
  1.3 31.9 %shard_map.86 = (bf16[128,1024]{1,0:T(8,128)(2,1)S(1)}, f32[16,1024]{1,0:T(8,128)S(1)}) custom-call(bf16[128,1024]{1,0:T(8,128)(2,1)} %g_hbm.1, bf16[1024,1024]{1,0:T(8,128)(2,1)} %ws_hbm.1, bf16[1024,1024]{1,0:T(8,128)(2,1)} %wn_hbm.1, bf16[1,8,128,128]{3,2,1,0:T(8,128)(2,1)} %adj_hbm.1, s32[1,8]{1,0:T(1,128)} %index_ref.1, s32[1,1]{1,0:T(1,128)} %bitcast.2.count_ref, ...), custom_call_target="tpu_custom_call" | custom-call | tf_op jit(solution)/shard_map/pallas_call | solution.py:407
  33.1 0.7 %shard_map.87 = (bf16[128,1024]{1,0:T(8,128)(2,1)}, f32[16,1024]{1,0:T(8,128)}) custom-call(bf16[128,1024]{1,0:T(8,128)(2,1)S(1)} %get-tuple-element.4.held_out, f32[16,1024]{1,0:T(8,128)S(1)} %get-tuple-element.5.held_prompt), custom_call_target="tpu_custom_call" | custom-call | tf_op jit(solution)/shard_map/pallas_call | solution.py:467
